TPU v7x, 32 devices: a whole 2x2x4 slice. The times are simulated.
32 devices in a mesh: dp: 8 (over z, y), tensor: 4 (over x, core).
Axes of the slice: x: 2, y: 2, z: 4, core: 2. Of those that a mesh axis runs over, the one named last changes fastest.
Arguments:
- stream_in: float32 [20480, 1024], P(('dp', 'tensor')), may hold values from -27 to 27
- segment_ids: int32 [20480], P('dp'), may hold values from 0 to 103, as said below
- parent_ids: int32 [20480], P('dp'), may hold values from 0 to 95, as said below
- norm_gain_attn: float32 [1024], replicated, may hold values from 0.5 to 1.5
- norm_shift_attn: float32 [1024], replicated, may hold values from -1 to 1
- norm_gain_mlp: float32 [1024], replicated, may hold values from 0.5 to 1.5
- norm_shift_mlp: float32 [1024], replicated, may hold values from -1 to 1
- qkv_weight: float32 [1024, 3072], P('dp', 'tensor'), may hold values from -0.1875 to 0.1875
- qkv_bias: float32 [3072], replicated, may hold values from -1 to 1
- dense_weight: float32 [1024, 1024], P('tensor', 'dp'), may hold values from -3 to 3
- dense_bias: float32 [1024], replicated, may hold values from -1 to 1
- fc_weight: float32 [1024, 4096], P('dp', 'tensor'), may hold values from -0.1875 to 0.1875
- fc_bias: float32 [4096], replicated, may hold values from -1 to 1
- out_weight: float32 [4096, 1024], P('tensor', 'dp'), may hold values from -0.125 to 0.125
- out_bias: float32 [1024], replicated, may hold values from -1 to 1
- out_grad: bfloat16 [20480, 1024], P(('dp', 'tensor')), may hold values from -6 to 6
Outputs:
- output: float32 [20480, 1024], P(('dp', 'tensor'))
- stream_grad: float32 [20480, 1024], P(('dp', 'tensor'))
- gain_attn_grad: float32 [1024], replicated
- shift_attn_grad: float32 [1024], replicated
- gain_mlp_grad: float32 [1024], replicated
- shift_mlp_grad: float32 [1024], replicated
- qkv_weight_grad: float32 [1024, 3072], P('dp', 'tensor')
- qkv_bias_grad: float32 [3072], replicated
- dense_weight_grad: float32 [1024, 1024], P('tensor', 'dp')
- dense_bias_grad: float32 [1024], replicated
- fc_weight_grad: float32 [1024, 4096], P('dp', 'tensor')
- fc_bias_grad: float32 [4096], replicated
- out_weight_grad: float32 [4096, 1024], P('tensor', 'dp')
- out_bias_grad: float32 [1024], replicated
- root_squares: float32 [3], replicated
Inputs may be any that keep to these rules, and one draw needn't show every extreme that they name: `segment_ids`: each tree is 2560 consecutive tokens: its trunk of 1024 tokens first, then 128-token branches and leaves in an order that varies; 4 branches with 2 leaves each; segment numbers are distinct across trees. `parent_ids`: A branch's parent is its tree's trunk, a leaf's parent a branch of the same tree.
All inputs are finite; a program needn't handle non-finite values.
Results may differ from a plain program's by a relative error of at most 0.012.
The roundings to bfloat16 on the way count: a program that leaves them out, or rounds other values in their place, can miss the bound.
Values may be sent and summed in bfloat16 or wider, within the bound.
No kernel may reach another device: no remote copies, remote signals or barrier semaphores. Data moves between devices by JAX's collectives and lax.ppermute only.
A program may use at most 320 MiB of HBM per device.

v0:
```python
import jax
import jax.numpy as jnp
from jax import lax
from jax.sharding import PartitionSpec as P

HD = 64
ROT = 16
TRUNK = 1024
SEG = 128
TREE = 2560
eps_norm = 1e-05
masked_score = -1e30


def contract_first(left, right):
    return lax.dot_general(
        left, right, (((0,), (0,)), ((), ())), preferred_element_type=jnp.float32
    )


def contract_last(left, right):
    return lax.dot_general(
        left, right, (((1,), (1,)), ((), ())), preferred_element_type=jnp.float32
    )


def group_products(left, right, groups):
    rows = left.shape[0]
    inner = left.shape[1] // groups
    parts = jnp.einsum(
        "rgc,gcd->grd",
        left.reshape(rows, groups, inner),
        right.reshape(groups, inner, right.shape[1]),
        preferred_element_type=jnp.float32,
    )
    return jnp.sum(parts.astype(jnp.bfloat16).astype(jnp.float32), axis=0)


def position_tables(segments, parents):
    token_count = segments.shape[0]
    index_all = jnp.arange(token_count, dtype=jnp.int32) % TREE
    root_ids = jnp.repeat(segments.reshape(token_count // TREE, TREE)[:, 0], TREE)
    depth_shift = jnp.where(parents == root_ids, 0, SEG)
    places = jnp.where(
        index_all < TRUNK, index_all, TRUNK + (index_all - TRUNK) % SEG + depth_shift
    )
    half_rot = ROT // 2
    inverse_freq = 10000.0 ** (-(jnp.arange(half_rot, dtype=jnp.float32) * 2.0 / ROT))
    angles = places.astype(jnp.float32)[:, None] * inverse_freq[None, :]
    cosine_table = jnp.concatenate([jnp.cos(angles), jnp.cos(angles)], axis=1)
    sine_table = jnp.concatenate([jnp.sin(angles), jnp.sin(angles)], axis=1)
    return (cosine_table, sine_table, root_ids)


def rotate_forward(field, cosine_table, sine_table):
    half_rot = ROT // 2
    turned_part = field[..., :ROT]
    first_half = turned_part[..., :half_rot]
    second_half = turned_part[..., half_rot:]
    swapped = jnp.concatenate([-second_half, first_half], axis=-1)
    turned = turned_part * cosine_table[:, None, :] + swapped * sine_table[:, None, :]
    return jnp.concatenate([turned, field[..., ROT:]], axis=-1)


def rotate_backward(gradient, cosine_table, sine_table):
    half_rot = ROT // 2
    turned_part = gradient[..., :ROT]
    with_cosine = turned_part * cosine_table[:, None, :]
    with_sine = turned_part * sine_table[:, None, :]
    back = with_cosine + jnp.concatenate(
        [with_sine[..., half_rot:], -with_sine[..., :half_rot]], axis=-1
    )
    return jnp.concatenate([back, gradient[..., ROT:]], axis=-1)


def visible(seg_rows, parent_rows, root_rows, index_rows, seg_cols, index_cols):
    same_seg = (seg_cols[None, :] == seg_rows[:, None]) & (
        index_cols[None, :] <= index_rows[:, None]
    )
    upper_seg = (seg_cols[None, :] == parent_rows[:, None]) & (parent_rows != seg_rows)[:, None]
    rooted_seg = (seg_cols[None, :] == root_rows[:, None]) & (root_rows != seg_rows)[:, None]
    return same_seg | upper_seg | rooted_seg


def block_size():
    return 512


def key_limit(row_end):
    return row_end if row_end <= TRUNK else TREE


def tree_scores(
    queries, key_rows, seg_tree, parent_tree, root_tree, row_start, block_rows, key_end
):
    index_tree = jnp.arange(TREE, dtype=jnp.int32)
    row_end = row_start + block_rows
    allowed = visible(
        seg_tree[row_start:row_end],
        parent_tree[row_start:row_end],
        root_tree[row_start:row_end],
        index_tree[row_start:row_end],
        seg_tree[:key_end],
        index_tree[:key_end],
    )
    raw_scores = jnp.einsum(
        "qhd,khd->hqk",
        queries[row_start:row_end],
        key_rows[:key_end],
        preferred_element_type=jnp.float32,
    )
    return jnp.where(allowed[None], raw_scores * HD ** (-0.5), masked_score)


def forward_tree(pieces):
    queries, key_rows, values, seg_tree, parent_tree, root_tree = pieces
    block_rows = block_size()
    context_parts = []
    total_parts = []
    for block_index in range(TREE // block_rows):
        row_start = block_index * block_rows
        key_end = key_limit(row_start + block_rows)
        scores = tree_scores(
            queries, key_rows, seg_tree, parent_tree, root_tree, row_start, block_rows, key_end
        )
        row_max = jnp.max(scores, axis=-1, keepdims=True)
        exp_total = jnp.sum(jnp.exp(scores - row_max), axis=-1, keepdims=True)
        log_total = row_max + jnp.log(exp_total)
        soft_low = jnp.exp(scores - log_total).astype(jnp.bfloat16)
        context_parts.append(
            jnp.einsum(
                "hqk,khd->qhd", soft_low, values[:key_end], preferred_element_type=jnp.float32
            )
        )
        total_parts.append(log_total[..., 0])
    return (jnp.concatenate(context_parts, axis=0), jnp.concatenate(total_parts, axis=1))


def backward_tree(pieces):
    queries, key_rows, values, seg_tree, parent_tree, root_tree, log_totals, grad_context = pieces
    block_rows = block_size()
    key_grad = jnp.zeros(key_rows.shape, jnp.float32)
    value_grad = jnp.zeros(values.shape, jnp.float32)
    query_parts = []
    for block_index in range(TREE // block_rows):
        row_start = block_index * block_rows
        row_end = row_start + block_rows
        key_end = key_limit(row_end)
        scores = tree_scores(
            queries, key_rows, seg_tree, parent_tree, root_tree, row_start, block_rows, key_end
        )
        soft_full = jnp.exp(scores - log_totals[:, row_start:row_end, None])
        soft_low = soft_full.astype(jnp.bfloat16)
        grad_rows = grad_context[row_start:row_end]
        value_grad = value_grad.at[:key_end].add(
            jnp.einsum("hqk,qhd->khd", soft_low, grad_rows, preferred_element_type=jnp.float32)
        )
        soft_grad = jnp.einsum(
            "qhd,khd->hqk", grad_rows, values[:key_end], preferred_element_type=jnp.float32
        )
        row_delta = jnp.sum(soft_full * soft_grad, axis=-1, keepdims=True)
        score_grad = (soft_full * (soft_grad - row_delta) * HD ** (-0.5)).astype(jnp.bfloat16)
        query_parts.append(
            jnp.einsum(
                "hqk,khd->qhd", score_grad, key_rows[:key_end], preferred_element_type=jnp.float32
            )
        )
        key_grad = key_grad.at[:key_end].add(
            jnp.einsum(
                "hqk,qhd->khd",
                score_grad,
                queries[row_start:row_end],
                preferred_element_type=jnp.float32,
            )
        )
    return (jnp.concatenate(query_parts, axis=0), key_grad, value_grad)


def local(
    stream_in,
    segment_ids,
    parent_ids,
    norm_gain_attn,
    norm_shift_attn,
    norm_gain_mlp,
    norm_shift_mlp,
    qkv_weight,
    qkv_bias,
    dense_weight,
    dense_bias,
    fc_weight,
    fc_bias,
    out_weight,
    out_bias,
    out_grad,
):
    tensor_rank = lax.axis_index("tensor")
    rows_local = stream_in.shape[0]
    group_rows = segment_ids.shape[0]
    qkv_width = qkv_weight.shape[1]
    heads_local = qkv_width // (3 * HD)
    ff_local = fc_weight.shape[1]
    tree_count = group_rows // TREE
    row_mean = jnp.mean(stream_in, axis=-1, keepdims=True)
    centred = stream_in - row_mean
    row_var = jnp.mean(centred * centred, axis=-1, keepdims=True)
    inv_std = lax.rsqrt(row_var + eps_norm)
    normalized = centred * inv_std
    sent_norm = normalized.astype(jnp.bfloat16)
    sent_group = lax.all_gather(sent_norm, "tensor", axis=0, tiled=True)
    qkv_whole, fc_whole, dense_whole, out_whole = (
        lax.all_gather(qkv_weight.astype(jnp.bfloat16), "dp", axis=0, tiled=True),
        lax.all_gather(fc_weight.astype(jnp.bfloat16), "dp", axis=0, tiled=True),
        lax.all_gather(dense_weight.astype(jnp.bfloat16), "dp", axis=1, tiled=True),
        lax.all_gather(out_weight.astype(jnp.bfloat16), "dp", axis=1, tiled=True),
    )
    sent_float = sent_group.astype(jnp.float32)
    normed_attn = (sent_float * norm_gain_attn + norm_shift_attn).astype(jnp.bfloat16)
    normed_mlp = (sent_float * norm_gain_mlp + norm_shift_mlp).astype(jnp.bfloat16)
    qkv_bias_local = lax.dynamic_slice_in_dim(qkv_bias, tensor_rank * qkv_width, qkv_width)
    fc_bias_local = lax.dynamic_slice_in_dim(fc_bias, tensor_rank * ff_local, ff_local)
    qkv = jnp.dot(normed_attn, qkv_whole, preferred_element_type=jnp.float32) + qkv_bias_local
    qkv = qkv.reshape(group_rows, heads_local, 3, HD)
    cosine_table, sine_table, root_ids = position_tables(segment_ids, parent_ids)
    queries = rotate_forward(qkv[:, :, 0], cosine_table, sine_table).astype(jnp.bfloat16)
    key_rows = rotate_forward(qkv[:, :, 1], cosine_table, sine_table).astype(jnp.bfloat16)
    values = qkv[:, :, 2].astype(jnp.bfloat16)
    tree_shape = (tree_count, TREE, heads_local, HD)
    tree_pieces = (
        queries.reshape(tree_shape),
        key_rows.reshape(tree_shape),
        values.reshape(tree_shape),
        segment_ids.reshape(tree_count, TREE),
        parent_ids.reshape(tree_count, TREE),
        root_ids.reshape(tree_count, TREE),
    )
    context, log_totals = lax.map(forward_tree, tree_pieces)
    context_low = context.reshape(group_rows, heads_local * HD).astype(jnp.bfloat16)
    hidden = jnp.dot(normed_mlp, fc_whole, preferred_element_type=jnp.float32) + fc_bias_local
    activated = jax.nn.gelu(hidden, approximate=False).astype(jnp.bfloat16)
    context_own, activated_own = (
        lax.all_to_all(context_low, "tensor", split_axis=0, concat_axis=1, tiled=True),
        lax.all_to_all(activated, "tensor", split_axis=0, concat_axis=1, tiled=True),
    )
    dense_every, out_every = (
        lax.all_gather(dense_whole, "tensor", axis=0, tiled=True),
        lax.all_gather(out_whole, "tensor", axis=0, tiled=True),
    )
    group_count = lax.axis_size("tensor")
    attn_sum = group_products(context_own, dense_every, group_count)
    mlp_sum = group_products(activated_own, out_every, group_count)
    attn_out = attn_sum + dense_bias
    mlp_out = mlp_sum + out_bias
    output = stream_in + attn_out + mlp_out
    grad_group = lax.all_gather(out_grad, "tensor", axis=0, tiled=True)
    grad_activated = contract_last(grad_group, out_whole)
    out_weight_part = contract_first(activated, grad_group)
    hidden_primal, gelu_pullback = jax.vjp(
        lambda field: jax.nn.gelu(field, approximate=False), hidden
    )
    grad_hidden = gelu_pullback(grad_activated)[0].astype(jnp.bfloat16)
    fc_bias_part = jnp.sum(grad_hidden.astype(jnp.float32), axis=0)
    fc_weight_part = contract_first(normed_mlp, grad_hidden)
    grad_normed_mlp = contract_last(grad_hidden, fc_whole)
    grad_context = contract_last(grad_group, dense_whole).astype(jnp.bfloat16)
    dense_weight_part = contract_first(context_low, grad_group)
    query_grad, key_grad, value_grad = lax.map(
        backward_tree, tree_pieces + (log_totals, grad_context.reshape(tree_shape))
    )
    query_grad = rotate_backward(
        query_grad.reshape(group_rows, heads_local, HD), cosine_table, sine_table
    )
    key_grad = rotate_backward(
        key_grad.reshape(group_rows, heads_local, HD), cosine_table, sine_table
    )
    value_grad = value_grad.reshape(group_rows, heads_local, HD)
    grad_qkv = jnp.stack([query_grad, key_grad, value_grad], axis=2).reshape(group_rows, qkv_width)
    grad_qkv = grad_qkv.astype(jnp.bfloat16)
    qkv_bias_part = jnp.sum(grad_qkv.astype(jnp.float32), axis=0)
    qkv_weight_part = contract_first(normed_attn, grad_qkv)
    grad_normed_attn = contract_last(grad_qkv, qkv_whole)
    gain_attn_part = jnp.sum(grad_normed_attn * sent_float, axis=0)
    shift_attn_part = jnp.sum(grad_normed_attn, axis=0)
    gain_mlp_part = jnp.sum(grad_normed_mlp * sent_float, axis=0)
    shift_mlp_part = jnp.sum(grad_normed_mlp, axis=0)
    grad_sent_part = grad_normed_attn * norm_gain_attn + grad_normed_mlp * norm_gain_mlp
    grad_sent = lax.psum_scatter(
        grad_sent_part.astype(jnp.bfloat16), "tensor", scatter_dimension=0, tiled=True
    ).astype(jnp.float32)
    mean_grad = jnp.mean(grad_sent, axis=-1, keepdims=True)
    mean_cross = jnp.mean(grad_sent * normalized, axis=-1, keepdims=True)
    stream_grad = out_grad.astype(jnp.float32) + inv_std * (
        grad_sent - mean_grad - normalized * mean_cross
    )
    qkv_weight_grad, fc_weight_grad, dense_weight_grad, out_weight_grad = (
        lax.psum_scatter(
            qkv_weight_part.astype(jnp.bfloat16), "dp", scatter_dimension=0, tiled=True
        ).astype(jnp.float32),
        lax.psum_scatter(
            fc_weight_part.astype(jnp.bfloat16), "dp", scatter_dimension=0, tiled=True
        ).astype(jnp.float32),
        lax.psum_scatter(
            dense_weight_part.astype(jnp.bfloat16), "dp", scatter_dimension=1, tiled=True
        ).astype(jnp.float32),
        lax.psum_scatter(
            out_weight_part.astype(jnp.bfloat16), "dp", scatter_dimension=1, tiled=True
        ).astype(jnp.float32),
    )
    residual_part = jnp.sum(out_grad.astype(jnp.float32), axis=0)
    qkv_bias_spread = lax.dynamic_update_slice(
        jnp.zeros(qkv_bias.shape, jnp.float32), qkv_bias_part, (tensor_rank * qkv_width,)
    )
    fc_bias_spread = lax.dynamic_update_slice(
        jnp.zeros(fc_bias.shape, jnp.float32), fc_bias_part, (tensor_rank * ff_local,)
    )
    (
        gain_attn_grad,
        shift_attn_grad,
        gain_mlp_grad,
        shift_mlp_grad,
        residual_grad,
        qkv_bias_grad,
        fc_bias_grad,
        output_square,
        attn_square,
        mlp_square,
    ) = lax.psum(
        (
            gain_attn_part,
            shift_attn_part,
            gain_mlp_part,
            shift_mlp_part,
            residual_part,
            qkv_bias_spread,
            fc_bias_spread,
            jnp.sum(output * output),
            jnp.sum(attn_out * attn_out),
            jnp.sum(mlp_out * mlp_out),
        ),
        ("dp", "tensor"),
    )
    count_all = float(
        rows_local * lax.axis_size("dp") * lax.axis_size("tensor") * stream_in.shape[1]
    )
    root_squares = jnp.sqrt(jnp.stack([output_square, attn_square, mlp_square]) / count_all)
    return (
        output,
        stream_grad,
        gain_attn_grad,
        shift_attn_grad,
        gain_mlp_grad,
        shift_mlp_grad,
        qkv_weight_grad,
        qkv_bias_grad,
        dense_weight_grad,
        residual_grad,
        fc_weight_grad,
        fc_bias_grad,
        out_weight_grad,
        residual_grad,
        root_squares,
    )


def solution(mesh):
    placed = (
        P(("dp", "tensor"), None),
        P("dp"),
        P("dp"),
        P(),
        P(),
        P(),
        P(),
        P("dp", "tensor"),
        P(),
        P("tensor", "dp"),
        P(),
        P("dp", "tensor"),
        P(),
        P("tensor", "dp"),
        P(),
        P(("dp", "tensor"), None),
    )
    return jax.shard_map(
        local,
        mesh=mesh,
        in_specs=placed,
        out_specs=(
            P(("dp", "tensor"), None),
            P(("dp", "tensor"), None),
            P(),
            P(),
            P(),
            P(),
            P("dp", "tensor"),
            P(),
            P("tensor", "dp"),
            P(),
            P("dp", "tensor"),
            P(),
            P("tensor", "dp"),
            P(),
            P(),
        ),
        check_vma=False,
    )
```

profile of v0, /device:TPU:0, one launch (start us, length us, event | category | flops | bytes accessed | tf_op | source)
XLA Modules:
  0.0 1078.6 jit_solution(15230396105723233312)
XLA Ops:
  18.3 33.0 %all_gather.26 = bf16[256,1024]{1,0:T(8,128)(2,1)} all-gather(bf16[256,128]{1,0:T(8,128)(2,1)S(1)} %convert_element_type.175), channel_id=1, replica_groups=mesh['dp'=8,'tensor'=4] {'dp'}, dimensions={1}, use_global_device_ids=true | all-gather | bytes 589824 | tf_op jit(solution)/shard_map/all_gather | solution.py:214
  68.8 34.1 %all-gather.8.cloned.1.call-done = bf16[2560,1024]{1,0:T(8,128)(2,1)} async-done(((bf16[640,1024]{1,0:T(8,128)(2,1)}), bf16[2560,1024]{1,0:T(8,128)(2,1)}) %all-gather.8.cloned.1.call-update) | async-done | bytes 5242896 | tf_op jit(solution)/shard_map/all_gather | solution.py:210
  116.5 28.5 %all-gather.20.cloned.1.call-done = bf16[2560,1024]{1,0:T(8,128)(2,1)} async-done(((bf16[640,1024]{1,0:T(8,128)(2,1)}), bf16[2560,1024]{1,0:T(8,128)(2,1)}) %all-gather.20.cloned.1.call-update) | async-done | bytes 5242896 | tf_op jit(solution)/shard_map/all_gather | solution.py:255
  198.5 18.0 %fusion.218 = f32[2560,4,64]{0,2,1:T(8,128)} fusion(f32[2560,4,64]{0,2,1:T(8,128)} %fusion.204, f32[4,512,1024]{2,1,0:T(8,128)} %fusion.248, f32[4,512,1024]{2,1,0:T(8,128)} %copy-done.2, f32[4,512]{1,0:T(4,128)S(1)} %log_add_fusion.3, pred[512,1024]{1,0:T(8,128)(4,1)S(1)} %and_or_fusion, bf16[2560,4,48]{0,2,1:T(8,128)(2,1)S(1)} %slice.741, ...), kind=kOutput, calls=%fused_computation.211 | convolution fusion | flops 292555776 | bytes 36454400 | tf_op jit(solution)/shard_map/while/body/eval_jaxpr/hqk,khd->qhd/dot_general | solution.py:164
  216.6 23.2 %fusion.197 = f32[2560,4,64]{0,2,1:T(8,128)} fusion(f32[2560,4,64]{0,2,1:T(8,128)} %scatter-add.14, f32[4,512,1024]{2,1,0:T(8,128)} %fusion.248, f32[4,512,1024]{2,1,0:T(8,128)} %copy-done.2, f32[4,512]{1,0:T(4,128)S(1)} %log_add_fusion.3, pred[512,1024]{1,0:T(8,128)(4,1)S(1)} %and_or_fusion, bf16[2560,4,48]{0,2,1:T(8,128)(2,1)S(1)} %slice.742, ...), kind=kOutput, calls=%fused_computation.187 | convolution fusion | flops 292293632 | bytes 38027264 | tf_op jit(solution)/shard_map/while/body/eval_jaxpr/hqk,qhd->khd/dot_general | solution.py:169
  306.5 40.6 %fusion.140 = f32[2560,4,64]{0,2,1:T(8,128)} fusion(f32[4,512,2560]{2,1,0:T(8,128)} %fusion.246, f32[4,512,2560]{2,1,0:T(8,128)} %copy-done.4, f32[4,512]{1,0:T(4,128)S(1)} %log_add_fusion.1, pred[512,2560]{1,0:T(8,128)(4,1)} %get-tuple-element.354, bf16[2560,4,48]{0,2,1:T(8,128)(2,1)S(1)} %slice.742, bf16[2560,4,16]{0,2,1:T(8,128)(2,1)S(1)} %get-tuple-element.341), kind=kOutput, calls=%fused_computation.132 | convolution fusion | flops 729289216 | bytes 90456064 | tf_op jit(solution)/shard_map/while/body/eval_jaxpr/hqk,qhd->khd/dot_general | solution.py:169
  347.1 38.3 %fusion.236 = f32[2560,4,64]{0,2,1:T(8,128)} fusion(f32[2560,4,64]{0,2,1:T(8,128)} %fusion.218, f32[4,512,2560]{2,1,0:T(8,128)} %fusion.247, f32[4,512,2560]{2,1,0:T(8,128)} %copy-done.5, f32[4,512]{1,0:T(4,128)S(1)} %log_add_fusion.2, pred[512,2560]{1,0:T(8,128)(4,1)} %get-tuple-element.353, bf16[2560,4,48]{0,2,1:T(8,128)(2,1)S(1)} %slice.741, ...), kind=kOutput, calls=%fused_computation.217 | convolution fusion | flops 731386368 | bytes 88358912 | tf_op jit(solution)/shard_map/while/body/eval_jaxpr/hqk,khd->qhd/dot_general | solution.py:164
  385.4 37.8 %fusion.230 = f32[2560,4,64]{0,2,1:T(8,128)} fusion(f32[2560,4,64]{0,2,1:T(8,128)} %fusion.236, f32[4,512,2560]{2,1,0:T(8,128)} %fusion.246, f32[4,512,2560]{2,1,0:T(8,128)} %copy-done.4, f32[4,512]{1,0:T(4,128)S(1)} %log_add_fusion.1, pred[512,2560]{1,0:T(8,128)(4,1)} %get-tuple-element.354, bf16[2560,4,48]{0,2,1:T(8,128)(2,1)S(1)} %slice.741, ...), kind=kOutput, calls=%fused_computation.215 | convolution fusion | flops 731386368 | bytes 88358912 | tf_op jit(solution)/shard_map/while/body/eval_jaxpr/hqk,khd->qhd/dot_general | solution.py:164
  423.2 40.6 %fusion.137 = f32[2560,4,64]{0,2,1:T(8,128)} fusion(bf16[512,4,64]{0,2,1:T(8,128)(2,1)S(1)} %copy-done.43, f32[4,512,2560]{2,1,0:T(8,128)} %fusion.245, f32[4,512,2560]{2,1,0:T(8,128)} %copy-done.3, f32[4,512]{1,0:T(4,128)S(1)} %log_add_fusion, pred[512,2560]{1,0:T(8,128)(4,1)} %get-tuple-element.352), kind=kOutput, calls=%fused_computation.131 | convolution fusion | flops 728764928 | bytes 46145536 | tf_op jit(solution)/shard_map/while/body/eval_jaxpr/hqk,qhd->khd/dot_general | solution.py:169
  463.8 37.8 %fusion.224 = f32[2560,4,64]{0,2,1:T(8,128)} fusion(f32[2560,4,64]{0,2,1:T(8,128)} %fusion.230, f32[4,512,2560]{2,1,0:T(8,128)} %fusion.245, f32[4,512,2560]{2,1,0:T(8,128)} %copy-done.3, f32[4,512]{1,0:T(4,128)S(1)} %log_add_fusion, pred[512,2560]{1,0:T(8,128)(4,1)} %get-tuple-element.352, bf16[2560,4,48]{0,2,1:T(8,128)(2,1)S(1)} %slice.741, ...), kind=kOutput, calls=%fused_computation.213 | convolution fusion | flops 731386368 | bytes 88358912 | tf_op jit(solution)/shard_map/while/body/eval_jaxpr/hqk,khd->qhd/dot_general | solution.py:164
  501.7 41.5 %fusion.156 = f32[2560,4,64]{0,2,1:T(8,128)} fusion(f32[2560,4,64]{0,2,1:T(8,128)} %fusion.137, f32[2560,4,64]{0,2,1:T(8,128)} %fusion.140, f32[2560,4,64]{0,2,1:T(8,128)} %fusion.197, f32[4,512,2560]{2,1,0:T(8,128)} %fusion.247, f32[4,512,2560]{2,1,0:T(8,128)} %copy-done.5, f32[4,512]{1,0:T(4,128)S(1)} %log_add_fusion.2, ...), kind=kOutput, calls=%fused_computation.143 | convolution fusion | flops 731255296 | bytes 98320384 | tf_op jit(solution)/shard_map/while/body/eval_jaxpr/hqk,qhd->khd/dot_general | solution.py:169
  559.7 11.7 %fusion.149 = f32[2560,4,64]{0,2,1:T(8,128)} fusion(f32[2560,4,64]{0,2,1:T(8,128)S(1)} %fusion.193, bf16[512,4,64]{0,2,1:T(8,128)(2,1)S(1)} %bitcast.184, f32[4,512,2560]{2,1,0:T(8,128)} %copy-done.5, f32[4,512]{1,0:T(4,128)S(1)} %log_add_fusion.2, pred[512,2560]{1,0:T(8,128)(4,1)S(1)} %copy-done.13), kind=kOutput, calls=%fused_computation.140 | convolution fusion | flops 692715520 | bytes 27795456 | tf_op jit(solution)/shard_map/while/body/eval_jaxpr/hqk,qhd->khd/dot_general | solution.py:156
  620.8 10.4 fusion.147
  644.4 11.2 %fusion.161 = f32[2560,1024]{1,0:T(8,128)} fusion(bf16[1024,1024]{1,0:T(8,128)(2,1)} %all-gather.14.cloned.1.call-done, bf16[2560,1024]{1,0:T(8,128)(2,1)} %all-gather.8.cloned.1.call-done, f32[1024]{0:T(1024)S(1)} %copy-done.60, f32[1024]{0:T(1024)S(1)} %copy-done.63), kind=kOutput, calls=%fused_computation.145 | convolution fusion | flops 5379194880 | bytes 17833984 | tf_op jit(solution)/shard_map/dot_general | solution.py:239
  655.6 33.9 %convert_reduce_fusion = (f32[1024]{0:T(1024)S(1)}, bf16[2560,1024]{1,0:T(8,128)(2,1)}, f32[2560,1024]{1,0:T(8,128)}) fusion(f32[2560,1024]{1,0:T(8,128)} %fusion.161, f32[1024]{0:T(1024)S(1)} %copy-done.51, bf16[2560,1024]{1,0:T(8,128)(2,1)} %all-gather.20.cloned.1.call-done, bf16[1024,1024]{1,0:T(8,128)(2,1)} %all-gather.16.cloned.1.call-done), kind=kOutput, calls=%fused_computation.47 | convolution fusion | flops 5565316096 | bytes 33562624 | tf_op jit(solution)/shard_map/dot_general | solution.py:22
  689.6 12.3 %multiply_convert_fusion.3 = bf16[2560,1024]{1,0:T(8,128)(2,1)} fusion(f32[2560,1024]{1,0:T(8,128)} %get-tuple-element.316, f32[2560,1024]{1,0:T(8,128)} %fusion.161, f32[1024]{0:T(1024)S(1)} %copy-done.51), kind=kLoop, calls=%fused_computation.51 | loop fusion | flops 10485760 | bytes 26218496 | tf_op jit(solution)/shard_map/convert_element_type | solution.py:240
  732.1 15.2 %fusion.328 = (f32[1024]{0:T(1024)S(1)}, f32[1024]{0:T(1024)S(1)}, bf16[2560,1024]{1,0:T(8,128)(2,1)}, f32[1024]{0:T(1024)S(1)}, f32[1024]{0:T(1024)S(1)}) fusion(bf16[2560,1024]{1,0:T(8,128)(2,1)} %all-gather.8.cloned.1.call-done, f32[1024]{0:T(1024)S(1)} %copy-done.63, f32[2560,1024]{1,0:T(8,128)S(1)} %fusion.336, f32[1024]{0:T(1024)S(1)} %copy-done.62, ...), kind=kOutput, calls=%fused_computation.332 | convolution fusion | flops 5397540864 | bytes 28336128 | tf_op jit(solution)/shard_map/dot_general | solution.py:22
  750.4 19.7 %all_to_all.29 = bf16[4,640,256]{2,1,0:T(8,128)(2,1)S(1)} all-to-all(bf16[4,640,256]{2,1,0:T(8,128)(2,1)S(1)} %copy.52), channel_id=1, replica_groups=mesh['dp'=8,'tensor'=4] {'tensor'}, dimensions={0} | all-to-all | bytes 2621440 | tf_op jit(solution)/shard_map/all_to_all | solution.py:242
  784.2 50.7 %reduce-scatter.18.cloned.1.call-done = bf16[128,1024]{1,0:T(8,128)(2,1)} async-done(((bf16[1024,1024]{1,0:T(8,128)(2,1)}), bf16[128,1024]{1,0:T(8,128)(2,1)}) %reduce-scatter.18.cloned.1.call-update) | async-done | bytes 262160
  836.9 69.0 %reduce-scatter.14.cloned.1.call-done = bf16[128,1024]{1,0:T(8,128)(2,1)} async-done(((bf16[1024,1024]{1,0:T(8,128)(2,1)}), bf16[128,1024]{1,0:T(8,128)(2,1)}) %reduce-scatter.14.cloned.1.call-update) | async-done | bytes 262160 | tf_op jit(solution)/shard_map/reduce_scatter | solution.py:299
  907.6 57.1 %all-gather.18.cloned.1.call-done = bf16[4096,1024]{1,0:T(8,128)(2,1)} async-done(((bf16[1024,1024]{1,0:T(8,128)(2,1)}), bf16[4096,1024]{1,0:T(8,128)(2,1)}) %all-gather.18.cloned.1.call-update) | async-done | bytes 8388624 | tf_op jit(solution)/shard_map/all_gather | solution.py:247
  964.7 11.9 %convert_reduce_fusion.1 = f32[640,1024]{1,0:T(8,128)} fusion(bf16[4,1024,1024]{2,1,0:T(8,128)(2,1)} %bitcast.191, bf16[4,640,1024]{2,1,0:T(8,128)(2,1)} %all-to-all-done.1), kind=kOutput, calls=%fused_computation.50 | convolution fusion | flops 5375918080 | bytes 16252928 | tf_op jit(solution)/shard_map/rgc,gcd->grd/dot_general | solution.py:30
  976.6 41.9 %reduce-scatter.10.cloned.1.call-done = bf16[640,1024]{1,0:T(8,128)(2,1)} async-done(((bf16[2560,1024]{1,0:T(8,128)(2,1)}), bf16[640,1024]{1,0:T(8,128)(2,1)}) %reduce-scatter.10.cloned.1.call-update) | async-done | bytes 1310736 | tf_op jit(solution)/shard_map/reduce_scatter | solution.py:287
  1027.6 40.9 %all-reduce.2 = (f32[1024]{0:T(1024)}, f32[1024]{0:T(1024)}, f32[1024]{0:T(1024)}, f32[1024]{0:T(1024)}, f32[3072]{0:T(1024)}, /*index=5*/f32[1024]{0:T(1024)S(1...) all-reduce(f32[1024]{0:T(1024)S(1)} %get-tuple-element.320, ...), channel_id=1, replica_groups=mesh['dp'=8,'tensor'=4] {'dp','tensor'}, use_global_device_ids=true, to_apply=%region_23.24 | all-reduce | flops 12291 | bytes 98328 | tf_op jit(solution)/shard_map/psum | solution.py:327
  (284 shorter events, 303.7 us)
Async XLA Ops:
  7.2 61.6 %all-gather.10.cloned.1.call-start = ((), (), s32[]{:S(2)}) async-start(), calls=%async_computation.8 | async-start | bytes 1769472 | tf_op jit(solution)/shard_map/all_gather | solution.py:212
  9.1 93.8 %all-gather.8.cloned.1.call-start = ((), (), s32[]{:S(2)}) async-start(), calls=%async_computation.7 | async-start | bytes 6553600 | tf_op jit(solution)/shard_map/all_gather | solution.py:210
  13.4 44.5 %copy-start.48 = (f32[640]{0:T(1024)}, f32[640]{0:T(1024)S(1)}, u32[]{:S(2)}) copy-start(f32[640]{0:T(1024)S(1)} %add_rsqrt_fusion) | copy-start | bytes 7684
  13.4 44.9 %slice-start.2 = ((s32[2560]{0:T(1024)}), s32[1024]{0:T(1024)S(1)}, s32[]{:S(2)}) async-start(s32[2560]{0:T(1024)} %param.49), calls=%async_computation.21 | async-start | bytes 8192 | tf_op jit(solution)/shard_map/while/body/eval_jaxpr/slice | solution.py:103
  14.8 88.1 %copy-start.58 = (f32[1024]{0:T(1024)S(1)}, f32[1024]{0:T(1024)}, u32[]{:S(2)}) copy-start(f32[1024]{0:T(1024)} %param.52) | copy-start | bytes 12292
  14.8 88.1 %copy-start.61 = (f32[1024]{0:T(1024)S(1)}, f32[1024]{0:T(1024)}, u32[]{:S(2)}) copy-start(f32[1024]{0:T(1024)} %param.51) | copy-start | bytes 12292
  14.8 130.1 %all-gather.20.cloned.1.call-start = ((), (), s32[]{:S(2)}) async-start(), calls=%async_computation.13 | async-start | bytes 6553600 | tf_op jit(solution)/shard_map/all_gather | solution.py:255
  15.6 628.8 %all-gather.14.cloned.1.call-start = ((), (), s32[]{:S(2)}) async-start(), calls=%async_computation.10 | async-start | bytes 2359296 | tf_op jit(solution)/shard_map/all_gather | solution.py:213
  16.4 639.3 %all-gather.16.cloned.1.call-start = ((), (), s32[]{:S(2)}) async-start(), calls=%async_computation.11 | async-start | bytes 2359296 | tf_op jit(solution)/shard_map/all_gather | solution.py:215
  18.2 757.9 %all-gather.12.cloned.1.call-start = ((), (), s32[]{:S(2)}) async-start(), calls=%async_computation.9 | async-start | bytes 2621440 | tf_op jit(solution)/shard_map/all_gather | solution.py:246
  51.3 729.6 %reduce-scatter.16.cloned.1.call-start = ((), (), s32[]{:S(2)}) async-start(), calls=%async_computation.17 | async-start | bytes 589824
  59.7 156.8 %copy-start.14 = (pred[512,1024]{1,0:T(8,128)(4,1)}, pred[512,1024]{1,0:T(8,128)(4,1)S(1)}, u32[]{:S(2)}) copy-start(pred[512,1024]{1,0:T(8,128)(4,1)S(1)} %and_or_fusion) | copy-start | bytes 1572868
  501.7 46.8 %copy-start.22 = (f32[2560,16]{0,1:T(8,128)S(1)}, f32[2560,16]{0,1:T(8,128)}, u32[]{:S(2)}) copy-start(f32[2560,16]{0,1:T(8,128)} %get-tuple-element.391) | copy-start | bytes 491524
  635.0 147.5 %reduce-scatter.12.cloned.1.call-start = ((), (), s32[]{:S(2)}) async-start(), calls=%async_computation.15 | async-start | bytes 1769472 | tf_op jit(solution)/shard_map/reduce_scatter | solution.py:296
  644.3 190.6 %reduce-scatter.18.cloned.1.call-start = ((), (), s32[]{:S(2)}) async-start(), calls=%async_computation.18 | async-start | bytes 2359296
  713.8 192.0 %reduce-scatter.14.cloned.1.call-start = ((), (), s32[]{:S(2)}) async-start(), calls=%async_computation.16 | async-start | bytes 2359296 | tf_op jit(solution)/shard_map/reduce_scatter | solution.py:299
  724.0 240.6 %all-gather.18.cloned.1.call-start = ((), (), s32[]{:S(2)}) async-start(), calls=%async_computation.12 | async-start | bytes 10485760 | tf_op jit(solution)/shard_map/all_gather | solution.py:247
  724.8 293.7 %reduce-scatter.10.cloned.1.call-start = ((), (), s32[]{:S(2)}) async-start(), calls=%async_computation.14 | async-start | bytes 6553600 | tf_op jit(solution)/shard_map/reduce_scatter | solution.py:287
  770.1 137.5 %all-to-all-start.1 = ((bf16[4,640,1024]{2,1,0:T(8,128)(2,1)}), bf16[4,640,1024]{2,1,0:T(8,128)(2,1)}, u32[]{:S(2)}, u32[]{:S(2)}) async-start(bf16[4,640,1024]{2,1,0:T(8,128)(2,1)} %bitcast.173), calls=%async_computation.1 | async-start | bytes 10485760 | tf_op jit(solution)/shard_map/all_to_all | solution.py:243
  964.7 53.8 %copy-start.1 = (f32[640,1024]{1,0:T(8,128)S(1)}, f32[640,1024]{1,0:T(8,128)}, u32[]{:S(2)}) copy-start(f32[640,1024]{1,0:T(8,128)} %param.48) | copy-start | bytes 7864324
  964.7 53.8 %copy-start.46 = (f32[640]{0:T(1024)S(1)}, f32[640]{0:T(1024)}, u32[]{:S(2)}) copy-start(f32[640]{0:T(1024)} %copy-done.45) | copy-start | bytes 7684
  964.7 53.8 %copy-start.49 = (f32[640]{0:T(1024)S(1)}, f32[640]{0:T(1024)}, u32[]{:S(2)}) copy-start(f32[640]{0:T(1024)} %copy-done.48) | copy-start | bytes 7684
  964.7 56.3 %copy-start.55 = (f32[1024]{0:T(1024)S(1)}, f32[1024]{0:T(1024)}, u32[]{:S(2)}) copy-start(f32[1024]{0:T(1024)} %param.62) | copy-start | bytes 12292
  964.7 56.3 %copy-start.56 = (f32[1024]{0:T(1024)S(1)}, f32[1024]{0:T(1024)}, u32[]{:S(2)}) copy-start(f32[1024]{0:T(1024)} %param.58) | copy-start | bytes 12292
  (59 other events, 455.1 us)
Sparse Core Ops, SparseCore 0:
  10.8 50.6 all-gather.9
  63.7 39.1 all-gather.7
  104.5 40.4 all-gather.19
  146.9 49.4 all-gather.13
  198.3 49.5 all-gather.15
  249.3 20.7 all-gather.11
  635.1 61.7 reduce-scatter.15
  700.7 63.8 reduce-scatter.11
  768.2 66.6 reduce-scatter.17
  838.9 66.9 reduce-scatter.13
  907.4 57.2 all-gather.17
  967.1 51.3 reduce-scatter.9
where the time goes:
time: 1080 us
  matrix products  555 us (51%)
  waiting for transfers between devices  283 us (26%)
  blocking collectives  93.6 us (9%)
  other arithmetic  88.5 us (8%)
  local copies, waits for them, and re-layouts  37.3 us (3%)
  between operations  15.5 us (1%)
    dot_general x5, matrix products, backward_tree(): jnp.einsum('hqk,qhd->khd', score_grad, queries[row_start:row_end], prefer...  155 us
    dot_general x5, matrix products, backward_tree(): jnp.einsum('hqk,khd->qhd', score_grad, key_rows[:key_end], preferred_elem...  142 us
    reduce_scatter x1, waiting for transfers between devices, local(): lax.psum_scatter(fc_weight_part.astype(jnp.bfloat16), 'dp', scatter_dimen...  69 us
    dot_general x4, matrix products, contract_last(): lax.dot_general(left, right, (((1,), (1,)), ((), ())), preferred_element_...  60.6 us
    all_gather x1, waiting for transfers between devices, local(): lax.all_gather(out_whole, 'tensor', axis=0, tiled=True)  57.1 us
    unnamed x14, waiting for transfers between devices  52.2 us
    reduce_scatter x1, waiting for transfers between devices, local(): lax.psum_scatter(grad_sent_part.astype(jnp.bfloat16), 'tensor', scatter_d...  41.9 us
    psum x1, blocking collectives, local(): lax.psum((gain_attn_part, shift_attn_part, gain_mlp_part, shift_mlp_part,...  40.9 us
  transfers between devices with their start and end apart: 13, of which 6 were waited for; matrix products, arithmetic and copies ran while one was open for 61% of the time, Pallas kernels for 0%

commit v1 on v0

--- a/solution.py
+++ b/solution.py
@@ -10,6 +10,18 @@
 TREE = 2560
 eps_norm = 1e-05
 masked_score = -1e30
+
+
+def doubled_up(x, axis, dim):
+    ways, here, step = (lax.axis_size(axis), lax.axis_index(axis), x.shape[dim])
+    line, have = (x, 1)
+    while have < ways:
+        line = jnp.concatenate(
+            [line, lax.ppermute(line, axis, [(d, (d - have) % ways) for d in range(ways)])],
+            axis=dim,
+        )
+        have = 2 * have
+    return jnp.roll(line, here * step, axis=dim)
 
 
 def contract_first(left, right):
@@ -211,7 +223,7 @@
     qkv_whole, fc_whole, dense_whole, out_whole = (
         lax.all_gather(qkv_weight.astype(jnp.bfloat16), "dp", axis=0, tiled=True),
         lax.all_gather(fc_weight.astype(jnp.bfloat16), "dp", axis=0, tiled=True),
-        lax.all_gather(dense_weight.astype(jnp.bfloat16), "dp", axis=1, tiled=True),
+        doubled_up(dense_weight.astype(jnp.bfloat16), "dp", 1),
         lax.all_gather(out_weight.astype(jnp.bfloat16), "dp", axis=1, tiled=True),
     )
     sent_float = sent_group.astype(jnp.float32)

time: 1080 us -> 1090 us (level)
  blocking collectives: 93.6 us -> 60.6 us
  waiting for transfers between devices: 283 us -> 313 us
    all_gather x1 -> x0, blocking collectives: 33 us -> none  [local(): lax.all_gather(dense_weight.astype(jnp.bfloat16), 'dp', axis=1, tiled=True)]
    ppermute x0 -> x3, waiting for transfers between devices: none -> 25.2 us  [doubled_up(): lax.ppermute(line, axis, [(d, (d - have) % ways) for d in range(ways)])]
  transfers between devices with their start and end apart: 13 -> 16, of which waited for: 6 -> 8; matrix products, arithmetic and copies ran while one was open for 61% -> 61% of each run, Pallas kernels for 0% -> 0%
where the time goes in v1:
time: 1090 us; the launch traced here: 1080 us
  matrix products  556 us (51%)
  waiting for transfers between devices  313 us (29%)
  other arithmetic  88.2 us (8%)
  blocking collectives  60.6 us (6%)
  local copies, waits for them, and re-layouts  38.2 us (4%)
  between operations  15.5 us (1%)
  starting transfers between devices  12.8 us (1%)
    dot_general x5, matrix products, backward_tree(): jnp.einsum('hqk,qhd->khd', score_grad, queries[row_start:row_end], prefer...  155 us
    dot_general x5, matrix products, backward_tree(): jnp.einsum('hqk,khd->qhd', score_grad, key_rows[:key_end], preferred_elem...  142 us
    reduce_scatter x1, waiting for transfers between devices, local(): lax.psum_scatter(fc_weight_part.astype(jnp.bfloat16), 'dp', scatter_dimen...  68.8 us
    dot_general x4, matrix products, contract_last(): lax.dot_general(left, right, (((1,), (1,)), ((), ())), preferred_element_...  60.7 us
    all_gather x1, waiting for transfers between devices, local(): lax.all_gather(out_whole, 'tensor', axis=0, tiled=True)  57.2 us
    unnamed x14, waiting for transfers between devices  52 us
    reduce_scatter x1, waiting for transfers between devices, local(): lax.psum_scatter(grad_sent_part.astype(jnp.bfloat16), 'tensor', scatter_d...  41.9 us
    psum x1, blocking collectives, local(): lax.psum((gain_attn_part, shift_attn_part, gain_mlp_part, shift_mlp_part,...  40.9 us
  transfers between devices with their start and end apart: 16, of which 8 were waited for; matrix products, arithmetic and copies ran while one was open for 61% of the time, Pallas kernels for 0%

profile of v1, /device:TPU:0, one launch (start us, length us, event | category | flops | bytes accessed | tf_op | source)
XLA Modules:
  0.0 1084.9 jit_solution(4160105223393051153)
XLA Ops:
  46.2 21.1 %collective-permute-done.2 = bf16[256,512]{1,0:T(8,128)(2,1)S(1)} collective-permute-done((bf16[256,512]{1,0:T(8,128)(2,1)S(1)}, bf16[256,512]{1,0:T(8,128)(2,1)S(1)}, u32[]{:S(2)}, u32[]{:S(2)}) %collective-permute-start.2) | collective-permute-done | bytes 262176 | tf_op jit(solution)/shard_map/ppermute | solution.py:20
  68.7 39.9 %all-gather.8.cloned.1.call-done = bf16[2560,1024]{1,0:T(8,128)(2,1)} async-done(((bf16[640,1024]{1,0:T(8,128)(2,1)}), bf16[2560,1024]{1,0:T(8,128)(2,1)}) %all-gather.8.cloned.1.call-update) | async-done | bytes 5242896 | tf_op jit(solution)/shard_map/all_gather | solution.py:222
  122.2 28.5 %all-gather.20.cloned.1.call-done = bf16[2560,1024]{1,0:T(8,128)(2,1)} async-done(((bf16[640,1024]{1,0:T(8,128)(2,1)}), bf16[2560,1024]{1,0:T(8,128)(2,1)}) %all-gather.20.cloned.1.call-update) | async-done | bytes 5242896 | tf_op jit(solution)/shard_map/all_gather | solution.py:267
  204.3 18.1 %fusion.219 = f32[2560,4,64]{0,2,1:T(8,128)} fusion(f32[2560,4,64]{0,2,1:T(8,128)} %fusion.205, f32[4,512,1024]{2,1,0:T(8,128)} %fusion.249, f32[4,512,1024]{2,1,0:T(8,128)} %copy-done.2, f32[4,512]{1,0:T(4,128)S(1)} %log_add_fusion.3, pred[512,1024]{1,0:T(8,128)(4,1)S(1)} %and_or_fusion, bf16[2560,4,48]{0,2,1:T(8,128)(2,1)S(1)} %slice.741, ...), kind=kOutput, calls=%fused_computation.212 | convolution fusion | flops 292555776 | bytes 36454400 | tf_op jit(solution)/shard_map/while/body/eval_jaxpr/hqk,khd->qhd/dot_general | solution.py:176
  222.4 23.3 %fusion.198 = f32[2560,4,64]{0,2,1:T(8,128)} fusion(f32[2560,4,64]{0,2,1:T(8,128)} %scatter-add.14, f32[4,512,1024]{2,1,0:T(8,128)} %fusion.249, f32[4,512,1024]{2,1,0:T(8,128)} %copy-done.2, f32[4,512]{1,0:T(4,128)S(1)} %log_add_fusion.3, pred[512,1024]{1,0:T(8,128)(4,1)S(1)} %and_or_fusion, bf16[2560,4,48]{0,2,1:T(8,128)(2,1)S(1)} %slice.742, ...), kind=kOutput, calls=%fused_computation.188 | convolution fusion | flops 292293632 | bytes 38027264 | tf_op jit(solution)/shard_map/while/body/eval_jaxpr/hqk,qhd->khd/dot_general | solution.py:181
  312.4 40.8 %fusion.140 = f32[2560,4,64]{0,2,1:T(8,128)} fusion(f32[4,512,2560]{2,1,0:T(8,128)} %fusion.247, f32[4,512,2560]{2,1,0:T(8,128)} %copy-done.4, f32[4,512]{1,0:T(4,128)S(1)} %log_add_fusion.1, pred[512,2560]{1,0:T(8,128)(4,1)} %get-tuple-element.356, bf16[2560,4,48]{0,2,1:T(8,128)(2,1)S(1)} %slice.742, bf16[2560,4,16]{0,2,1:T(8,128)(2,1)S(1)} %get-tuple-element.343), kind=kOutput, calls=%fused_computation.132 | convolution fusion | flops 729289216 | bytes 90456064 | tf_op jit(solution)/shard_map/while/body/eval_jaxpr/hqk,qhd->khd/dot_general | solution.py:181
  353.2 38.3 %fusion.237 = f32[2560,4,64]{0,2,1:T(8,128)} fusion(f32[2560,4,64]{0,2,1:T(8,128)} %fusion.219, f32[4,512,2560]{2,1,0:T(8,128)} %fusion.248, f32[4,512,2560]{2,1,0:T(8,128)} %copy-done.5, f32[4,512]{1,0:T(4,128)S(1)} %log_add_fusion.2, pred[512,2560]{1,0:T(8,128)(4,1)} %get-tuple-element.355, bf16[2560,4,48]{0,2,1:T(8,128)(2,1)S(1)} %slice.741, ...), kind=kOutput, calls=%fused_computation.218 | convolution fusion | flops 731386368 | bytes 88358912 | tf_op jit(solution)/shard_map/while/body/eval_jaxpr/hqk,khd->qhd/dot_general | solution.py:176
  391.5 38.0 %fusion.231 = f32[2560,4,64]{0,2,1:T(8,128)} fusion(f32[2560,4,64]{0,2,1:T(8,128)} %fusion.237, f32[4,512,2560]{2,1,0:T(8,128)} %fusion.247, f32[4,512,2560]{2,1,0:T(8,128)} %copy-done.4, f32[4,512]{1,0:T(4,128)S(1)} %log_add_fusion.1, pred[512,2560]{1,0:T(8,128)(4,1)} %get-tuple-element.356, bf16[2560,4,48]{0,2,1:T(8,128)(2,1)S(1)} %slice.741, ...), kind=kOutput, calls=%fused_computation.216 | convolution fusion | flops 731386368 | bytes 88358912 | tf_op jit(solution)/shard_map/while/body/eval_jaxpr/hqk,khd->qhd/dot_general | solution.py:176
  429.5 40.7 %fusion.137 = f32[2560,4,64]{0,2,1:T(8,128)} fusion(bf16[512,4,64]{0,2,1:T(8,128)(2,1)S(1)} %copy-done.43, f32[4,512,2560]{2,1,0:T(8,128)} %fusion.246, f32[4,512,2560]{2,1,0:T(8,128)} %copy-done.3, f32[4,512]{1,0:T(4,128)S(1)} %log_add_fusion, pred[512,2560]{1,0:T(8,128)(4,1)} %get-tuple-element.354), kind=kOutput, calls=%fused_computation.131 | convolution fusion | flops 728764928 | bytes 46145536 | tf_op jit(solution)/shard_map/while/body/eval_jaxpr/hqk,qhd->khd/dot_general | solution.py:181
  470.2 37.9 %fusion.225 = f32[2560,4,64]{0,2,1:T(8,128)} fusion(f32[2560,4,64]{0,2,1:T(8,128)} %fusion.231, f32[4,512,2560]{2,1,0:T(8,128)} %fusion.246, f32[4,512,2560]{2,1,0:T(8,128)} %copy-done.3, f32[4,512]{1,0:T(4,128)S(1)} %log_add_fusion, pred[512,2560]{1,0:T(8,128)(4,1)} %get-tuple-element.354, bf16[2560,4,48]{0,2,1:T(8,128)(2,1)S(1)} %slice.741, ...), kind=kOutput, calls=%fused_computation.214 | convolution fusion | flops 731386368 | bytes 88358912 | tf_op jit(solution)/shard_map/while/body/eval_jaxpr/hqk,khd->qhd/dot_general | solution.py:176
  508.1 41.6 %fusion.156 = f32[2560,4,64]{0,2,1:T(8,128)} fusion(f32[2560,4,64]{0,2,1:T(8,128)} %fusion.137, f32[2560,4,64]{0,2,1:T(8,128)} %fusion.140, f32[2560,4,64]{0,2,1:T(8,128)} %fusion.198, f32[4,512,2560]{2,1,0:T(8,128)} %fusion.248, f32[4,512,2560]{2,1,0:T(8,128)} %copy-done.5, f32[4,512]{1,0:T(4,128)S(1)} %log_add_fusion.2, ...), kind=kOutput, calls=%fused_computation.143 | convolution fusion | flops 731255296 | bytes 98320384 | tf_op jit(solution)/shard_map/while/body/eval_jaxpr/hqk,qhd->khd/dot_general | solution.py:181
  566.3 11.7 %fusion.149 = f32[2560,4,64]{0,2,1:T(8,128)} fusion(f32[2560,4,64]{0,2,1:T(8,128)S(1)} %fusion.194, bf16[512,4,64]{0,2,1:T(8,128)(2,1)S(1)} %bitcast.186, f32[4,512,2560]{2,1,0:T(8,128)} %copy-done.5, f32[4,512]{1,0:T(4,128)S(1)} %log_add_fusion.2, pred[512,2560]{1,0:T(8,128)(4,1)S(1)} %copy-done.13), kind=kOutput, calls=%fused_computation.140 | convolution fusion | flops 692715520 | bytes 27795456 | tf_op jit(solution)/shard_map/while/body/eval_jaxpr/hqk,qhd->khd/dot_general | solution.py:168
  627.4 10.4 fusion.147
  651.0 11.2 %fusion.161 = f32[2560,1024]{1,0:T(8,128)} fusion(bf16[1024,1024]{1,0:T(8,128)(2,1)} %all-gather.14.cloned.1.call-done, bf16[2560,1024]{1,0:T(8,128)(2,1)} %all-gather.8.cloned.1.call-done, f32[1024]{0:T(1024)S(1)} %copy-done.60, f32[1024]{0:T(1024)S(1)} %copy-done.63), kind=kOutput, calls=%fused_computation.145 | convolution fusion | flops 5379194880 | bytes 17833984 | tf_op jit(solution)/shard_map/dot_general | solution.py:251
  662.2 33.9 %convert_reduce_fusion = (f32[1024]{0:T(1024)S(1)}, bf16[2560,1024]{1,0:T(8,128)(2,1)}, f32[2560,1024]{1,0:T(8,128)}) fusion(f32[2560,1024]{1,0:T(8,128)} %fusion.161, f32[1024]{0:T(1024)S(1)} %copy-done.51, bf16[2560,1024]{1,0:T(8,128)(2,1)} %all-gather.20.cloned.1.call-done, bf16[1024,1024]{1,0:T(8,128)(2,1)} %all-gather.16.cloned.1.call-done), kind=kOutput, calls=%fused_computation.47 | convolution fusion | flops 5565316096 | bytes 33562624 | tf_op jit(solution)/shard_map/dot_general | solution.py:34
  696.1 12.3 %multiply_convert_fusion.3 = bf16[2560,1024]{1,0:T(8,128)(2,1)} fusion(f32[2560,1024]{1,0:T(8,128)} %get-tuple-element.316, f32[2560,1024]{1,0:T(8,128)} %fusion.161, f32[1024]{0:T(1024)S(1)} %copy-done.51), kind=kLoop, calls=%fused_computation.51 | loop fusion | flops 10485760 | bytes 26218496 | tf_op jit(solution)/shard_map/convert_element_type | solution.py:252
  738.7 15.2 %fusion.329 = (f32[1024]{0:T(1024)S(1)}, f32[1024]{0:T(1024)S(1)}, bf16[2560,1024]{1,0:T(8,128)(2,1)}, f32[1024]{0:T(1024)S(1)}, f32[1024]{0:T(1024)S(1)}) fusion(bf16[2560,1024]{1,0:T(8,128)(2,1)} %all-gather.8.cloned.1.call-done, f32[1024]{0:T(1024)S(1)} %copy-done.63, f32[2560,1024]{1,0:T(8,128)S(1)} %fusion.337, f32[1024]{0:T(1024)S(1)} %copy-done.62, ...), kind=kOutput, calls=%fused_computation.344 | convolution fusion | flops 5397540864 | bytes 28336128 | tf_op jit(solution)/shard_map/dot_general | solution.py:34
  757.0 19.7 %all_to_all.29 = bf16[4,640,256]{2,1,0:T(8,128)(2,1)S(1)} all-to-all(bf16[4,640,256]{2,1,0:T(8,128)(2,1)S(1)} %copy.52), channel_id=1, replica_groups=mesh['dp'=8,'tensor'=4] {'tensor'}, dimensions={0} | all-to-all | bytes 2621440 | tf_op jit(solution)/shard_map/all_to_all | solution.py:254
  790.8 50.5 %reduce-scatter.18.cloned.1.call-done = bf16[128,1024]{1,0:T(8,128)(2,1)} async-done(((bf16[1024,1024]{1,0:T(8,128)(2,1)}), bf16[128,1024]{1,0:T(8,128)(2,1)}) %reduce-scatter.18.cloned.1.call-update) | async-done | bytes 262160
  843.3 68.8 %reduce-scatter.14.cloned.1.call-done = bf16[128,1024]{1,0:T(8,128)(2,1)} async-done(((bf16[1024,1024]{1,0:T(8,128)(2,1)}), bf16[128,1024]{1,0:T(8,128)(2,1)}) %reduce-scatter.14.cloned.1.call-update) | async-done | bytes 262160 | tf_op jit(solution)/shard_map/reduce_scatter | solution.py:311
  913.8 57.2 %all-gather.18.cloned.1.call-done = bf16[4096,1024]{1,0:T(8,128)(2,1)} async-done(((bf16[1024,1024]{1,0:T(8,128)(2,1)}), bf16[4096,1024]{1,0:T(8,128)(2,1)}) %all-gather.18.cloned.1.call-update) | async-done | bytes 8388624 | tf_op jit(solution)/shard_map/all_gather | solution.py:259
  971.0 11.9 %convert_reduce_fusion.1 = f32[640,1024]{1,0:T(8,128)} fusion(bf16[4,1024,1024]{2,1,0:T(8,128)(2,1)} %bitcast.193, bf16[4,640,1024]{2,1,0:T(8,128)(2,1)} %all-to-all-done.1), kind=kOutput, calls=%fused_computation.50 | convolution fusion | flops 5375918080 | bytes 16252928 | tf_op jit(solution)/shard_map/rgc,gcd->grd/dot_general | solution.py:42
  982.9 41.9 %reduce-scatter.10.cloned.1.call-done = bf16[640,1024]{1,0:T(8,128)(2,1)} async-done(((bf16[2560,1024]{1,0:T(8,128)(2,1)}), bf16[640,1024]{1,0:T(8,128)(2,1)}) %reduce-scatter.10.cloned.1.call-update) | async-done | bytes 1310736 | tf_op jit(solution)/shard_map/reduce_scatter | solution.py:299
  1033.9 40.9 %all-reduce.2 = (f32[1024]{0:T(1024)}, f32[1024]{0:T(1024)}, f32[1024]{0:T(1024)}, f32[1024]{0:T(1024)}, f32[3072]{0:T(1024)}, /*index=5*/f32[1024]{0:T(1024)S(1...) all-reduce(f32[1024]{0:T(1024)S(1)} %get-tuple-element.322, ...), channel_id=1, replica_groups=mesh['dp'=8,'tensor'=4] {'dp','tensor'}, use_global_device_ids=true, to_apply=%region_23.24 | all-reduce | flops 12291 | bytes 98328 | tf_op jit(solution)/shard_map/psum | solution.py:339
  (299 shorter events, 315.5 us)
Async XLA Ops:
  7.2 61.5 %all-gather.10.cloned.1.call-start = ((), (), s32[]{:S(2)}) async-start(), calls=%async_computation.8 | async-start | bytes 1769472 | tf_op jit(solution)/shard_map/all_gather | solution.py:224
  9.1 99.5 %all-gather.8.cloned.1.call-start = ((), (), s32[]{:S(2)}) async-start(), calls=%async_computation.7 | async-start | bytes 6553600 | tf_op jit(solution)/shard_map/all_gather | solution.py:222
  14.8 135.8 %all-gather.20.cloned.1.call-start = ((), (), s32[]{:S(2)}) async-start(), calls=%async_computation.13 | async-start | bytes 6553600 | tf_op jit(solution)/shard_map/all_gather | solution.py:267
  15.5 635.4 %all-gather.14.cloned.1.call-start = ((), (), s32[]{:S(2)}) async-start(), calls=%async_computation.10 | async-start | bytes 2359296 | tf_op jit(solution)/shard_map/all_gather | solution.py:225
  16.3 645.9 %all-gather.16.cloned.1.call-start = ((), (), s32[]{:S(2)}) async-start(), calls=%async_computation.11 | async-start | bytes 2359296 | tf_op jit(solution)/shard_map/all_gather | solution.py:227
  16.4 21.3 %collective-permute-start = (bf16[256,128]{1,0:T(8,128)(2,1)S(1)}, bf16[256,128]{1,0:T(8,128)(2,1)S(1)}, u32[]{:S(2)}, u32[]{:S(2)}) collective-permute-start(bf16[256,128]{1,0:T(8,128)(2,1)S(1)} %get-tuple-element.320), channel_id=1, source_target_pairs={{0,28},{4,0},{8,4},{12,8},{16,12},{20,16},{24,20},{28,24},{1,29},{... | collective-permute-start | bytes 196616 | tf_op jit(solution)/shard_map/ppermute | solution.py:20
  24.3 84.3 %copy-start.58 = (f32[1024]{0:T(1024)S(1)}, f32[1024]{0:T(1024)}, u32[]{:S(2)}) copy-start(f32[1024]{0:T(1024)} %param.52) | copy-start | bytes 12292
  24.3 84.3 %copy-start.61 = (f32[1024]{0:T(1024)S(1)}, f32[1024]{0:T(1024)}, u32[]{:S(2)}) copy-start(f32[1024]{0:T(1024)} %param.51) | copy-start | bytes 12292
  24.3 758.4 %all-gather.12.cloned.1.call-start = ((), (), s32[]{:S(2)}) async-start(), calls=%async_computation.9 | async-start | bytes 2621440 | tf_op jit(solution)/shard_map/all_gather | solution.py:258
  37.8 5.7 collective-permute-start.1
  39.4 183.0 %copy-start.14 = (pred[512,1024]{1,0:T(8,128)(4,1)}, pred[512,1024]{1,0:T(8,128)(4,1)S(1)}, u32[]{:S(2)}) copy-start(pred[512,1024]{1,0:T(8,128)(4,1)S(1)} %and_or_fusion) | copy-start | bytes 1572868
  43.5 23.8 %collective-permute-start.2 = (bf16[256,512]{1,0:T(8,128)(2,1)S(1)}, bf16[256,512]{1,0:T(8,128)(2,1)S(1)}, u32[]{:S(2)}, u32[]{:S(2)}) collective-permute-start(bf16[256,512]{1,0:T(8,128)(2,1)S(1)} %pad_maximum_fusion.4), channel_id=1, source_target_pairs={{0,16},{4,20},{8,24},{12,28},{16,0},{20,4},{24,8},{28,12},{1,17},{... | collective-permute-start | bytes 786440 | tf_op jit(solution)/shard_map/ppermute | solution.py:20
  68.3 719.2 %reduce-scatter.16.cloned.1.call-start = ((), (), s32[]{:S(2)}) async-start(), calls=%async_computation.17 | async-start | bytes 589824
  641.6 147.6 %reduce-scatter.12.cloned.1.call-start = ((), (), s32[]{:S(2)}) async-start(), calls=%async_computation.15 | async-start | bytes 1769472 | tf_op jit(solution)/shard_map/reduce_scatter | solution.py:308
  650.9 190.4 %reduce-scatter.18.cloned.1.call-start = ((), (), s32[]{:S(2)}) async-start(), calls=%async_computation.18 | async-start | bytes 2359296
  720.4 191.6 %reduce-scatter.14.cloned.1.call-start = ((), (), s32[]{:S(2)}) async-start(), calls=%async_computation.16 | async-start | bytes 2359296 | tf_op jit(solution)/shard_map/reduce_scatter | solution.py:311
  730.6 240.3 %all-gather.18.cloned.1.call-start = ((), (), s32[]{:S(2)}) async-start(), calls=%async_computation.12 | async-start | bytes 10485760 | tf_op jit(solution)/shard_map/all_gather | solution.py:259
  731.4 293.4 %reduce-scatter.10.cloned.1.call-start = ((), (), s32[]{:S(2)}) async-start(), calls=%async_computation.14 | async-start | bytes 6553600 | tf_op jit(solution)/shard_map/reduce_scatter | solution.py:299
  776.7 137.1 %all-to-all-start.1 = ((bf16[4,640,1024]{2,1,0:T(8,128)(2,1)}), bf16[4,640,1024]{2,1,0:T(8,128)(2,1)}, u32[]{:S(2)}, u32[]{:S(2)}) async-start(bf16[4,640,1024]{2,1,0:T(8,128)(2,1)} %bitcast.175), calls=%async_computation.1 | async-start | bytes 10485760 | tf_op jit(solution)/shard_map/all_to_all | solution.py:255
  971.0 53.8 %copy-start.1 = (f32[640,1024]{1,0:T(8,128)S(1)}, f32[640,1024]{1,0:T(8,128)}, u32[]{:S(2)}) copy-start(f32[640,1024]{1,0:T(8,128)} %param.48) | copy-start | bytes 7864324
  971.0 53.8 %copy-start.46 = (f32[640]{0:T(1024)S(1)}, f32[640]{0:T(1024)}, u32[]{:S(2)}) copy-start(f32[640]{0:T(1024)} %copy-done.45) | copy-start | bytes 7684
  971.0 53.8 %copy-start.49 = (f32[640]{0:T(1024)S(1)}, f32[640]{0:T(1024)}, u32[]{:S(2)}) copy-start(f32[640]{0:T(1024)} %copy-done.48) | copy-start | bytes 7684
  971.0 56.3 %copy-start.55 = (f32[1024]{0:T(1024)S(1)}, f32[1024]{0:T(1024)}, u32[]{:S(2)}) copy-start(f32[1024]{0:T(1024)} %param.62) | copy-start | bytes 12292
  971.0 56.3 %copy-start.56 = (f32[1024]{0:T(1024)S(1)}, f32[1024]{0:T(1024)}, u32[]{:S(2)}) copy-start(f32[1024]{0:T(1024)} %param.58) | copy-start | bytes 12292
  (62 other events, 496.8 us)
Sparse Core Ops, SparseCore 0:
  10.8 56.6 all-gather.9
  69.6 38.9 all-gather.7
  110.2 40.4 all-gather.19
  152.6 49.3 all-gather.13
  203.9 49.5 all-gather.15
  255.5 20.7 all-gather.11
  641.7 61.8 reduce-scatter.15
  707.4 63.7 reduce-scatter.11
  774.7 66.5 reduce-scatter.17
  845.2 66.7 reduce-scatter.13
  913.6 57.3 all-gather.17
  973.4 51.3 reduce-scatter.9
